TPU v7x, 32 devices: a whole 2x2x4 slice. The times are simulated.
32 devices in a mesh: dp: 4 (over z), adapter: 2 (over x), fsdp: 4 (over y, core).
Axes of the slice: x: 2, y: 2, z: 4, core: 2. Of those that a mesh axis runs over, the one named last changes fastest.
Arguments:
- adapter_index: int32 [768], P(('dp', 'adapter', 'fsdp')), may hold values from 0 to 1, as said below
- output_gradient: bfloat16 [768, 4096], P(('dp', 'adapter', 'fsdp')), may hold values from -6 to 6
- hidden: bfloat16 [768, 14336], P(('dp', 'adapter', 'fsdp')), may hold values from -6 to 6
- frozen_down_weight: bfloat16 [14336, 4096], P('adapter', 'fsdp'), may hold values from -0.046875 to 0.046875
- adapter_input_maps: bfloat16 [2, 16, 14336], P('adapter'), may hold values from -0.046875 to 0.046875
- adapter_output_maps: bfloat16 [2, 16, 4096], P('adapter'), may hold values from -1.5 to 1.5
Outputs:
- hidden_gradient: bfloat16 [768, 14336], P(('dp', 'adapter', 'fsdp'))
- adapter_input_gradient: float32 [2, 16, 14336], P('adapter')
- adapter_output_gradient: float32 [2, 16, 4096], P('adapter')
Inputs may be any that keep to these rules, and one draw needn't show every extreme that they name: `adapter_index`: adapter i sits at index i // 1 of adapter. Of the 24 tokens of one device (aligned blocks of 24 rows), at most 12 name adapters at the same index; in every draw one index is named by exactly 12 tokens of every device.
All inputs are finite; a program needn't handle non-finite values.
Results may differ from a plain program's by a relative error of at most 0.015.
Values may be sent and summed in bfloat16 or wider, within the bound.
A program may use at most 64 MiB of HBM per device.

v0:
```python
import jax
import jax.numpy as jnp
from jax import lax
from jax.sharding import PartitionSpec as P

adapter_scale = 2.0


def on_device(
    adapter_index,
    output_gradient,
    hidden,
    frozen_down_weight,
    adapter_input_maps,
    adapter_output_maps,
):
    tok_rows = output_gradient.shape[0]
    token_tenants = lax.axis_size("adapter")
    fibres = lax.axis_size("fsdp")
    groups = lax.axis_size("dp")
    tenant_token_count = adapter_input_maps.shape[0]
    adapter_rank_size = adapter_input_maps.shape[1]
    hidden_units_width = hidden.shape[1]
    model_dimension_width = output_gradient.shape[1]
    capacity = max(2, min(tok_rows // 2, 2 * tok_rows // token_tenants))
    every_token = tok_rows * token_tenants * fibres * groups
    scaling_factor = adapter_scale * (tenant_token_count * token_tenants) / every_token
    slab_width = frozen_down_weight.shape[1]
    own_columns = lax.all_to_all(output_gradient, "fsdp", split_axis=1, concat_axis=0, tiled=True)
    spread = lax.all_gather(own_columns, "adapter", axis=0, tiled=True)
    blocks = spread.reshape(token_tenants, fibres, tok_rows, slab_width)
    per_fibre = token_tenants * tok_rows
    taken = blocks
    taken = jnp.transpose(taken, (1, 0, 2, 3)).reshape(
        per_fibre * lax.axis_size("fsdp"), slab_width
    )
    partial_base = lax.psum_scatter(
        lax.dot_general(
            taken, frozen_down_weight, (((1,), (1,)), ((), ())), preferred_element_type=jnp.float32
        ).astype(jnp.bfloat16),
        "fsdp",
        scatter_dimension=0,
        tiled=True,
    )
    frozen_term = lax.all_to_all(partial_base, "adapter", split_axis=0, concat_axis=1, tiled=True)
    owner_of = adapter_index // tenant_token_count
    local_of = adapter_index - owner_of * tenant_token_count
    same_owner = owner_of[:, None] == owner_of[None, :]
    earlier = jnp.arange(tok_rows)[None, :] < jnp.arange(tok_rows)[:, None]
    position = jnp.sum((same_owner & earlier).astype(jnp.int32), axis=1)
    slot_of = owner_of * capacity + position
    slot_count = token_tenants * capacity
    placing = (jnp.arange(slot_count, dtype=jnp.int32)[:, None] == slot_of[None, :]).astype(
        jnp.bfloat16
    )
    send_out = jnp.dot(placing, output_gradient, preferred_element_type=jnp.float32).astype(
        jnp.bfloat16
    )
    send_hidden = jnp.dot(placing, hidden, preferred_element_type=jnp.float32).astype(jnp.bfloat16)
    send_tag = jnp.dot(
        placing, (local_of + 1).astype(jnp.bfloat16), preferred_element_type=jnp.float32
    ).astype(jnp.bfloat16)
    recv_out, recv_hidden, recv_tag = (
        lax.all_to_all(send_out, "adapter", split_axis=0, concat_axis=0, tiled=True),
        lax.all_to_all(send_hidden, "adapter", split_axis=0, concat_axis=0, tiled=True),
        lax.all_to_all(send_tag, "adapter", split_axis=0, concat_axis=0, tiled=True),
    )
    flattened_input_map = adapter_input_maps.reshape(
        tenant_token_count * adapter_rank_size, hidden_units_width
    )
    flattened_output_map = adapter_output_maps.reshape(
        tenant_token_count * adapter_rank_size, model_dimension_width
    )
    chosen = (
        recv_tag.astype(jnp.float32)[:, None]
        == (jnp.arange(tenant_token_count) + 1).astype(jnp.float32)[None, :]
    )
    row_mask = jnp.repeat(chosen, adapter_rank_size, axis=1).astype(jnp.float32)
    multiplier = (
        lax.dot_general(
            recv_out,
            flattened_output_map,
            (((1,), (1,)), ((), ())),
            preferred_element_type=jnp.float32,
        )
        * row_mask
    ).astype(jnp.bfloat16)
    low_rank = (
        lax.dot_general(
            recv_hidden,
            flattened_input_map,
            (((1,), (1,)), ((), ())),
            preferred_element_type=jnp.float32,
        )
        * row_mask
    ).astype(jnp.bfloat16)
    adapter_token_rows = (
        adapter_scale * jnp.dot(multiplier, flattened_input_map, preferred_element_type=jnp.float32)
    ).astype(jnp.bfloat16)
    grad_a_part = lax.dot_general(
        multiplier, recv_hidden, (((0,), (0,)), ((), ())), preferred_element_type=jnp.float32
    )
    grad_b_part = lax.dot_general(
        low_rank, recv_out, (((0,), (0,)), ((), ())), preferred_element_type=jnp.float32
    )
    backward_result = lax.all_to_all(
        adapter_token_rows, "adapter", split_axis=0, concat_axis=0, tiled=True
    )
    adapter_selection = lax.dot_general(
        placing, backward_result, (((0,), (0,)), ((), ())), preferred_element_type=jnp.float32
    )
    hidden_gradient = (frozen_term.astype(jnp.float32) + adapter_selection).astype(jnp.bfloat16)
    input_map_total, output_map_total = (
        lax.psum(grad_a_part.astype(jnp.bfloat16), ("dp", "fsdp")).astype(jnp.float32),
        lax.psum(grad_b_part.astype(jnp.bfloat16), ("dp", "fsdp")).astype(jnp.float32),
    )
    adapter_input_gradient = (scaling_factor * input_map_total).reshape(
        tenant_token_count, adapter_rank_size, hidden_units_width
    )
    adapter_output_gradient = (scaling_factor * output_map_total).reshape(
        tenant_token_count, adapter_rank_size, model_dimension_width
    )
    return (hidden_gradient, adapter_input_gradient, adapter_output_gradient)


def solution(mesh):
    in_specs = (
        P(("dp", "adapter", "fsdp")),
        P(("dp", "adapter", "fsdp"), None),
        P(("dp", "adapter", "fsdp"), None),
        P("adapter", "fsdp"),
        P("adapter", None, None),
        P("adapter", None, None),
    )
    out_specs = (
        P(("dp", "adapter", "fsdp"), None),
        P("adapter", None, None),
        P("adapter", None, None),
    )
    return jax.shard_map(
        on_device, mesh=mesh, in_specs=in_specs, out_specs=out_specs, check_vma=False
    )
```

profile of v0, /device:TPU:0, one launch (start us, length us, event | category | flops | bytes accessed | tf_op | source)
XLA Modules:
  0.0 185.1 jit_solution(1483464234489830159)
XLA Ops:
  8.0 0.9 convert_reduce_fusion
  9.0 0.7 multiply_add_fusion
  9.6 0.1 fusion.4
  9.8 0.7 all_to_all.71
  10.4 4.2 %all-to-all-start.2 = ((bf16[2,12,1]{1,2,0:T(2,128)(2,1)}), bf16[2,12,1]{1,2,0:T(2,128)(2,1)S(1)}, u32[]{:S(2)}, u32[]{:S(2)}) async-start(bf16[2,12,1]{1,2,0:T(2,128)(2,1)} %all_to_all.71), calls=%async_computation.3 | async-start | bytes 2048 | tf_op jit(solution)/shard_map/all_to_all | solution.py:66
  14.6 1.1 convolution_convert_fusion.3
  15.8 0.8 all_to_all.62
  16.5 1.8 all-to-all-done.2
  18.3 3.4 %all-to-all-start.3 = ((bf16[2,12,4096]{2,1,0:T(8,128)(2,1)}), bf16[2,12,4096]{2,1,0:T(8,128)(2,1)S(1)}, u32[]{:S(2)}, u32[]{:S(2)}) async-start(bf16[2,12,4096]{2,1,0:T(8,128)(2,1)} %all_to_all.62), calls=%async_computation.4 | async-start | bytes 524288 | tf_op jit(solution)/shard_map/all_to_all | solution.py:64
  21.8 0.7 copy.30
  22.5 4.5 %all-to-all-done.3 = bf16[2,12,4096]{2,1,0:T(8,128)(2,1)S(1)} async-done(((bf16[2,12,4096]{2,1,0:T(8,128)(2,1)}), bf16[2,12,4096]{2,1,0:T(8,128)(2,1)S(1)}, u32[]{:S(2)}, u32[]{:S(2)}) %all-to-all-start.3) | async-done | bytes 196640 | tf_op jit(solution)/shard_map/all_to_all | solution.py:64
  27.0 3.4 %all-to-all-start = ((bf16[24,4,1024]{2,0,1:T(8,128)(2,1)}), bf16[24,4,1024]{2,0,1:T(8,128)(2,1)S(1)}, u32[]{:S(2)}, u32[]{:S(2)}) async-start(bf16[24,4,1024]{2,0,1:T(8,128)(2,1)} %bitcast.43), calls=%async_computation | async-start | bytes 393216 | tf_op jit(solution)/shard_map/all_to_all | solution.py:29
  30.3 0.3 convolution_convert_fusion
  30.7 1.1 all_to_all.68
  31.8 3.8 %all-to-all-done = bf16[24,4,1024]{2,0,1:T(8,128)(2,1)S(1)} async-done(((bf16[24,4,1024]{2,0,1:T(8,128)(2,1)}), bf16[24,4,1024]{2,0,1:T(8,128)(2,1)S(1)}, u32[]{:S(2)}, u32[]{:S(2)}) %all-to-all-start) | async-done | bytes 196640 | tf_op jit(solution)/shard_map/all_to_all | solution.py:29
  35.6 3.6 %all-to-all-start.5 = ((bf16[2,12,14336]{2,1,0:T(8,128)(2,1)}), bf16[2,12,14336]{2,1,0:T(8,128)(2,1)S(1)}, u32[]{:S(2)}, u32[]{:S(2)}) async-start(bf16[2,12,14336]{2,1,0:T(8,128)(2,1)} %all_to_all.68), calls=%async_computation.6 | async-start | bytes 1835008 | tf_op jit(solution)/shard_map/all_to_all | solution.py:65
  39.4 0.2 fusion.2
  39.6 15.7 %all_gather.3 = bf16[192,1024]{1,0:T(8,128)(2,1)S(1)} all-gather(bf16[96,1024]{1,0:T(8,128)(2,1)S(1)} %bitcast.47), channel_id=1, replica_groups=mesh['dp'=4,'adapter'=2,'fsdp'=4] {'adapter'}, dimensions={0}, use_global_device_ids=true | all-gather | bytes 589824 | tf_op jit(solution)/shard_map/all_gather | solution.py:30
  55.3 0.2 all_to_all.70
  55.5 1.1 convolution_convert_fusion.1
  56.6 1.2 convolution_convert_fusion.4
  57.9 11.7 %convolution_convert_fusion.2 = bf16[192,7168]{1,0:T(8,128)(2,1)} fusion(bf16[192,1024]{1,0:T(8,128)(2,1)S(1)} %bitcast.49, bf16[7168,1024]{1,0:T(8,128)(2,1)} %param.9), kind=kOutput, calls=%fused_computation.6 | convolution fusion | flops 2819948544 | bytes 17825792 | tf_op jit(solution)/shard_map/dot_general | solution.py:38
  69.6 0.4 fusion
  70.0 0.2 all_to_all.65
  70.2 13.5 %all_to_all.78 = bf16[2,12,14336]{2,1,0:T(8,128)(2,1)S(1)} all-to-all(bf16[2,12,14336]{2,1,0:T(8,128)(2,1)S(1)} %all_to_all.65), channel_id=1, replica_groups=mesh['dp'=4,'adapter'=2,'fsdp'=4] {'adapter'}, dimensions={0} | all-to-all | bytes 1376256 | tf_op jit(solution)/shard_map/all_to_all | solution.py:106
  83.7 0.2 all_to_all.67
  83.9 77.5 %all-reduce.3.cloned.1.call-done = (bf16[16,14336]{1,0:T(8,128)(2,1)}, bf16[16,4096]{1,0:T(8,128)(2,1)}) async-done(((bf16[16,14336]{1,0:T(8,128)(2,1)}, bf16[16,4096]{1,0:T(8,128)(2,1)}), (bf16[16,14336]{1,0:T(8,128)(2,1)}, bf16[16,4096]{1,0:T(8,128)(2,1)})) %all-reduce.3.cloned.1.call-update) | async-done | bytes 589840 | tf_op jit(solution)/shard_map/psum | solution.py:114
  161.4 2.0 %multiply_bitcast_fusion = f32[1,16,14336]{2,1,0:T(8,128)} fusion(bf16[16,14336]{1,0:T(8,128)(2,1)} %get-tuple-element.3), kind=kLoop, calls=%fused_computation.16 | loop fusion | flops 458752 | bytes 1376256 | tf_op jit(solution)/shard_map/reshape | solution.py:117
  163.4 3.5 %all-to-all-start.1 = ((bf16[2,24,7168]{2,1,0:T(8,128)(2,1)}), bf16[2,24,7168]{2,1,0:T(8,128)(2,1)S(1)}, u32[]{:S(2)}, u32[]{:S(2)}) async-start(bf16[2,24,7168]{2,1,0:T(8,128)(2,1)} %bitcast.48), calls=%async_computation.2 | async-start | bytes 1376256 | tf_op jit(solution)/shard_map/all_to_all | solution.py:45
  167.0 0.7 multiply_bitcast_fusion.1
  167.7 8.5 %all-to-all-done.1 = bf16[2,24,7168]{2,1,0:T(8,128)(2,1)S(1)} async-done(((bf16[2,24,7168]{2,1,0:T(8,128)(2,1)}), bf16[2,24,7168]{2,1,0:T(8,128)(2,1)S(1)}, u32[]{:S(2)}, u32[]{:S(2)}) %all-to-all-start.1) | async-done | bytes 688160 | tf_op jit(solution)/shard_map/all_to_all | solution.py:45
  176.4 1.2 fusion.1
  (22 shorter events, 0.5 us)
Async XLA Ops:
  8.0 22.3 %copy-start = (bf16[24,14336]{1,0:T(8,128)(2,1)S(1)}, bf16[24,14336]{1,0:T(8,128)(2,1)}, u32[]{:S(2)}) copy-start(bf16[24,14336]{1,0:T(8,128)(2,1)} %param.8) | copy-start | bytes 2064388
  8.0 13.8 %copy-start.2 = (bf16[24,4096]{1,0:T(8,128)(2,1)S(1)}, bf16[24,4096]{1,0:T(8,128)(2,1)}, u32[]{:S(2)}) copy-start(bf16[24,4096]{1,0:T(8,128)(2,1)} %param.7) | copy-start | bytes 589828
  10.4 7.9 %all-to-all-start.2 = ((bf16[2,12,1]{1,2,0:T(2,128)(2,1)}), bf16[2,12,1]{1,2,0:T(2,128)(2,1)S(1)}, u32[]{:S(2)}, u32[]{:S(2)}) async-start(bf16[2,12,1]{1,2,0:T(2,128)(2,1)} %all_to_all.71), calls=%async_computation.3 | async-start | bytes 2048 | tf_op jit(solution)/shard_map/all_to_all | solution.py:66
  18.3 8.6 %all-to-all-start.3 = ((bf16[2,12,4096]{2,1,0:T(8,128)(2,1)}), bf16[2,12,4096]{2,1,0:T(8,128)(2,1)S(1)}, u32[]{:S(2)}, u32[]{:S(2)}) async-start(bf16[2,12,4096]{2,1,0:T(8,128)(2,1)} %all_to_all.62), calls=%async_computation.4 | async-start | bytes 524288 | tf_op jit(solution)/shard_map/all_to_all | solution.py:64
  27.0 8.6 %all-to-all-start = ((bf16[24,4,1024]{2,0,1:T(8,128)(2,1)}), bf16[24,4,1024]{2,0,1:T(8,128)(2,1)S(1)}, u32[]{:S(2)}, u32[]{:S(2)}) async-start(bf16[24,4,1024]{2,0,1:T(8,128)(2,1)} %bitcast.43), calls=%async_computation | async-start | bytes 393216 | tf_op jit(solution)/shard_map/all_to_all | solution.py:29
  31.8 7.6 %copy-start.4 = (bf16[1,16,4096]{2,1,0:T(8,128)(2,1)S(1)}, bf16[1,16,4096]{2,1,0:T(8,128)(2,1)}, u32[]{:S(2)}) copy-start(bf16[1,16,4096]{2,1,0:T(8,128)(2,1)} %param.11) | copy-start | bytes 393220
  35.6 19.7 %all-to-all-start.5 = ((bf16[2,12,14336]{2,1,0:T(8,128)(2,1)}), bf16[2,12,14336]{2,1,0:T(8,128)(2,1)S(1)}, u32[]{:S(2)}, u32[]{:S(2)}) async-start(bf16[2,12,14336]{2,1,0:T(8,128)(2,1)} %all_to_all.68), calls=%async_computation.6 | async-start | bytes 1835008 | tf_op jit(solution)/shard_map/all_to_all | solution.py:65
  39.2 122.2 %all-reduce.3.cloned.1.call-start = ((), (), s32[]{:S(2)}) async-start(), calls=%async_computation.8 | async-start | bytes 1179648 | tf_op jit(solution)/shard_map/psum | solution.py:114
  55.3 1.3 copy-start.1
  57.8 105.6 %reduce-scatter.2.cloned.1.call-start = ((), (), s32[]{:S(2)}) async-start(), calls=%async_computation.7 | async-start | bytes 3440640 | tf_op jit(solution)/shard_map/reduce_scatter | solution.py:37
  161.4 5.6 %copy-start.3 = (bf16[16,4096]{1,0:T(8,128)(2,1)S(1)}, bf16[16,4096]{1,0:T(8,128)(2,1)}, u32[]{:S(2)}) copy-start(bf16[16,4096]{1,0:T(8,128)(2,1)} %get-tuple-element.4) | copy-start | bytes 393220
  163.4 12.8 %all-to-all-start.1 = ((bf16[2,24,7168]{2,1,0:T(8,128)(2,1)}), bf16[2,24,7168]{2,1,0:T(8,128)(2,1)S(1)}, u32[]{:S(2)}, u32[]{:S(2)}) async-start(bf16[2,24,7168]{2,1,0:T(8,128)(2,1)} %bitcast.48), calls=%async_computation.2 | async-start | bytes 1376256 | tf_op jit(solution)/shard_map/all_to_all | solution.py:45
Sparse Core Ops, SparseCore 0:
  58.0 103.3 all-reduce.2
Sparse Core Ops, SparseCore 1:
  69.7 35.7 reduce-scatter.1
where the time goes:
time: 186 us; the launch traced here: 185 us
  waiting for transfers between devices  96.1 us (52%)
  blocking collectives  29.2 us (16%)
  starting transfers between devices  18.2 us (10%)
  matrix products  17.3 us (9%)
  between operations  15.6 us (8%)
  other arithmetic  4.49 us (2%)
  local copies, waits for them, and re-layouts  4.02 us (2%)
    psum x1, waiting for transfers between devices, on_device(): lax.psum(grad_a_part.astype(jnp.bfloat16), ('dp', 'fsdp'))  77.5 us
    all_gather x1, blocking collectives, on_device(): spread = lax.all_gather(own_columns, 'adapter', axis=0, tiled=True)  15.7 us
    all_to_all x1, blocking collectives, on_device(): lax.all_to_all(adapter_token_rows, 'adapter', split_axis=0, concat_axis=0...  13.5 us
    dot_general x1, matrix products, on_device(): lax.dot_general(taken, frozen_down_weight, (((1,), (1,)), ((), ())), pref...  11.7 us
    all_to_all x1, waiting for transfers between devices, on_device(): lax.all_to_all(partial_base, 'adapter', split_axis=0, concat_axis=1, tile...  8.49 us
    all_to_all x1, waiting for transfers between devices, on_device(): lax.all_to_all(send_out, 'adapter', split_axis=0, concat_axis=0, tiled=True)  4.46 us
    all_to_all x1, starting transfers between devices, on_device(): lax.all_to_all(send_tag, 'adapter', split_axis=0, concat_axis=0, tiled=True)  4.23 us
    all_to_all x1, waiting for transfers between devices, on_device(): lax.all_to_all(output_gradient, 'fsdp', split_axis=1, concat_axis=0, tile...  3.82 us
  transfers between devices with their start and end apart: 7, of which 5 were waited for; matrix products, arithmetic and copies ran while one was open for 9% of the time, Pallas kernels for 0%

commit v1 on v0

--- a/solution.py
+++ b/solution.py
@@ -110,8 +110,9 @@
         placing, backward_result, (((0,), (0,)), ((), ())), preferred_element_type=jnp.float32
     )
     hidden_gradient = (frozen_term.astype(jnp.float32) + adapter_selection).astype(jnp.bfloat16)
+    desk_close = lambda values: lax.psum(lax.psum(values, "fsdp"), "dp")
     input_map_total, output_map_total = (
-        lax.psum(grad_a_part.astype(jnp.bfloat16), ("dp", "fsdp")).astype(jnp.float32),
+        desk_close(grad_a_part.astype(jnp.bfloat16)).astype(jnp.float32),
         lax.psum(grad_b_part.astype(jnp.bfloat16), ("dp", "fsdp")).astype(jnp.float32),
     )
     adapter_input_gradient = (scaling_factor * input_map_total).reshape(

time: 186 us -> 271 us (1.46)
  waiting for transfers between devices: 96.1 us -> 192 us
  blocking collectives: 29.2 us -> 15.7 us
  starting transfers between devices: 18.2 us -> 21.8 us
    psum x1 -> x3, waiting for transfers between devices: 77.5 us -> 144 us  [the longest x1 92.2 us: on_device(): lax.psum(grad_b_part.astype(jnp.bfloat16), ('dp', 'fsdp'))]
    reduce_scatter x1, waiting for transfers between devices: 0.01 us -> 37.7 us  [on_device(): lax.psum_scatter(lax.dot_general(taken, frozen_down_weight, (((1,), (1,))...]
    all_to_all x1 -> x0, blocking collectives: 13.5 us -> none  [on_device(): lax.all_to_all(adapter_token_rows, 'adapter', split_axis=0, concat_axis=0...]
    all_to_all x1, waiting for transfers between devices: 8.49 us -> 0.01 us  [on_device(): lax.all_to_all(partial_base, 'adapter', split_axis=0, concat_axis=1, tile...]
    all_to_all x0 -> x1, starting transfers between devices: none -> 3.56 us  [on_device(): lax.all_to_all(adapter_token_rows, 'adapter', split_axis=0, concat_axis=0...]
  transfers between devices with their start and end apart: 7 -> 10, of which waited for: 5 -> 7; matrix products, arithmetic and copies ran while one was open for 9% -> 7% of each run, Pallas kernels for 0% -> 0%
where the time goes in v1:
time: 271 us
  waiting for transfers between devices  192 us (71%)
  starting transfers between devices  21.8 us (8%)
  matrix products  17.4 us (6%)
  blocking collectives  15.7 us (6%)
  between operations  13.9 us (5%)
  other arithmetic  5.36 us (2%)
  local copies, waits for them, and re-layouts  4.94 us (2%)
    psum x1, waiting for transfers between devices, on_device(): lax.psum(grad_b_part.astype(jnp.bfloat16), ('dp', 'fsdp'))  92.2 us
    psum x2, waiting for transfers between devices, on_device(): desk_close = lambda values: lax.psum(lax.psum(values, 'fsdp'), 'dp')  51.5 us
    reduce_scatter x1, waiting for transfers between devices, on_device(): lax.psum_scatter(lax.dot_general(taken, frozen_down_weight, (((1,), (1,))...  37.7 us
    all_gather x1, blocking collectives, on_device(): spread = lax.all_gather(own_columns, 'adapter', axis=0, tiled=True)  15.7 us
    dot_general x1, matrix products, on_device(): lax.dot_general(taken, frozen_down_weight, (((1,), (1,)), ((), ())), pref...  11.8 us
  transfers between devices with their start and end apart: 10, of which 7 were waited for; matrix products, arithmetic and copies ran while one was open for 7% of the time, Pallas kernels for 0%

profile of v1, /device:TPU:0, one launch (start us, length us, event | category | flops | bytes accessed | tf_op | source)
XLA Modules:
  0.0 270.7 jit_solution(2769618833912638409)
XLA Ops:
  7.2 0.9 convert_reduce_fusion
  8.1 0.7 multiply_add_fusion
  8.9 0.7 all_to_all.71
  9.6 4.2 %all-to-all-start.2 = ((bf16[2,12,1]{1,2,0:T(2,128)(2,1)}), bf16[2,12,1]{1,2,0:T(2,128)(2,1)S(1)}, u32[]{:S(2)}, u32[]{:S(2)}) async-start(bf16[2,12,1]{1,2,0:T(2,128)(2,1)} %all_to_all.71), calls=%async_computation.3 | async-start | bytes 2048 | tf_op jit(solution)/shard_map/all_to_all | solution.py:66
  13.8 1.1 convolution_convert_fusion.3
  14.9 0.8 all_to_all.62
  15.7 1.8 all-to-all-done.2
  17.5 3.4 %all-to-all-start.3 = ((bf16[2,12,4096]{2,1,0:T(8,128)(2,1)}), bf16[2,12,4096]{2,1,0:T(8,128)(2,1)S(1)}, u32[]{:S(2)}, u32[]{:S(2)}) async-start(bf16[2,12,4096]{2,1,0:T(8,128)(2,1)} %all_to_all.62), calls=%async_computation.4 | async-start | bytes 524288 | tf_op jit(solution)/shard_map/all_to_all | solution.py:64
  21.0 0.7 copy.30
  21.7 4.5 %all-to-all-done.3 = bf16[2,12,4096]{2,1,0:T(8,128)(2,1)S(1)} async-done(((bf16[2,12,4096]{2,1,0:T(8,128)(2,1)}), bf16[2,12,4096]{2,1,0:T(8,128)(2,1)S(1)}, u32[]{:S(2)}, u32[]{:S(2)}) %all-to-all-start.3) | async-done | bytes 196640 | tf_op jit(solution)/shard_map/all_to_all | solution.py:64
  26.1 3.4 %all-to-all-start = ((bf16[24,4,1024]{2,0,1:T(8,128)(2,1)}), bf16[24,4,1024]{2,0,1:T(8,128)(2,1)S(1)}, u32[]{:S(2)}, u32[]{:S(2)}) async-start(bf16[24,4,1024]{2,0,1:T(8,128)(2,1)} %bitcast.43), calls=%async_computation | async-start | bytes 393216 | tf_op jit(solution)/shard_map/all_to_all | solution.py:29
  29.5 0.3 convolution_convert_fusion
  29.8 1.1 all_to_all.68
  30.9 3.8 %all-to-all-done = bf16[24,4,1024]{2,0,1:T(8,128)(2,1)S(1)} async-done(((bf16[24,4,1024]{2,0,1:T(8,128)(2,1)}), bf16[24,4,1024]{2,0,1:T(8,128)(2,1)S(1)}, u32[]{:S(2)}, u32[]{:S(2)}) %all-to-all-start) | async-done | bytes 196640 | tf_op jit(solution)/shard_map/all_to_all | solution.py:29
  34.8 3.6 %all-to-all-start.5 = ((bf16[2,12,14336]{2,1,0:T(8,128)(2,1)}), bf16[2,12,14336]{2,1,0:T(8,128)(2,1)S(1)}, u32[]{:S(2)}, u32[]{:S(2)}) async-start(bf16[2,12,14336]{2,1,0:T(8,128)(2,1)} %all_to_all.68), calls=%async_computation.6 | async-start | bytes 1835008 | tf_op jit(solution)/shard_map/all_to_all | solution.py:65
  38.6 0.2 fusion.2
  38.7 15.7 %all_gather.3 = bf16[192,1024]{1,0:T(8,128)(2,1)S(1)} all-gather(bf16[96,1024]{1,0:T(8,128)(2,1)S(1)} %bitcast.47), channel_id=1, replica_groups=mesh['dp'=4,'adapter'=2,'fsdp'=4] {'adapter'}, dimensions={0}, use_global_device_ids=true | all-gather | bytes 589824 | tf_op jit(solution)/shard_map/all_gather | solution.py:30
  54.5 0.2 all_to_all.70
  54.7 1.1 convolution_convert_fusion.1
  55.8 1.2 convolution_convert_fusion.4
  57.1 11.8 %convolution_convert_fusion.2 = bf16[192,7168]{1,0:T(8,128)(2,1)} fusion(bf16[192,1024]{1,0:T(8,128)(2,1)S(1)} %bitcast.49, bf16[7168,1024]{1,0:T(8,128)(2,1)} %param.9), kind=kOutput, calls=%fused_computation.6 | convolution fusion | flops 2819948544 | bytes 17825792 | tf_op jit(solution)/shard_map/dot_general | solution.py:38
  68.9 0.4 fusion
  69.3 1.1 all_to_all.65
  70.4 3.6 %all-to-all-start.4 = ((bf16[2,12,14336]{2,1,0:T(8,128)(2,1)}), bf16[2,12,14336]{2,1,0:T(8,128)(2,1)S(1)}, u32[]{:S(2)}, u32[]{:S(2)}) async-start(bf16[2,12,14336]{2,1,0:T(8,128)(2,1)} %all_to_all.65), calls=%async_computation.5 | async-start | bytes 1835008 | tf_op jit(solution)/shard_map/all_to_all | solution.py:106
  74.0 15.2 %all-reduce.4.cloned.1.call-done = bf16[16,14336]{1,0:T(8,128)(2,1)} async-done(((bf16[16,14336]{1,0:T(8,128)(2,1)}), bf16[16,14336]{1,0:T(8,128)(2,1)}) %all-reduce.4.cloned.1.call-update) | async-done | bytes 458768 | tf_op jit(solution)/shard_map/psum | solution.py:113
  89.3 92.2 %all-reduce.8.cloned.1.call-done = bf16[16,4096]{1,0:T(8,128)(2,1)} async-done(((bf16[16,4096]{1,0:T(8,128)(2,1)}), bf16[16,4096]{1,0:T(8,128)(2,1)}) %all-reduce.8.cloned.1.call-update) | async-done | bytes 131088 | tf_op jit(solution)/shard_map/psum | solution.py:116
  181.5 1.6 multiply_bitcast_fusion.1
  183.3 37.7 %reduce-scatter.2.cloned.1.call-done = bf16[48,7168]{1,0:T(8,128)(2,1)} async-done(((bf16[192,7168]{1,0:T(8,128)(2,1)}), bf16[48,7168]{1,0:T(8,128)(2,1)}) %reduce-scatter.2.cloned.1.call-update) | async-done | bytes 688144 | tf_op jit(solution)/shard_map/reduce_scatter | solution.py:37
  221.0 3.5 %all-to-all-start.1 = ((bf16[2,24,7168]{2,1,0:T(8,128)(2,1)}), bf16[2,24,7168]{2,1,0:T(8,128)(2,1)S(1)}, u32[]{:S(2)}, u32[]{:S(2)}) async-start(bf16[2,24,7168]{2,1,0:T(8,128)(2,1)} %bitcast.48), calls=%async_computation.2 | async-start | bytes 1376256 | tf_op jit(solution)/shard_map/all_to_all | solution.py:45
  224.5 36.3 %all-reduce.6.cloned.1.call-done = bf16[16,14336]{1,0:T(8,128)(2,1)} async-done(((bf16[16,14336]{1,0:T(8,128)(2,1)}), bf16[16,14336]{1,0:T(8,128)(2,1)}) %all-reduce.6.cloned.1.call-update) | async-done | bytes 458768 | tf_op jit(solution)/shard_map/psum | solution.py:113
  260.8 2.0 multiply_bitcast_fusion
  263.0 1.2 fusion.1
  (27 shorter events, 0.9 us)
Async XLA Ops:
  7.2 22.3 %copy-start = (bf16[24,14336]{1,0:T(8,128)(2,1)S(1)}, bf16[24,14336]{1,0:T(8,128)(2,1)}, u32[]{:S(2)}) copy-start(bf16[24,14336]{1,0:T(8,128)(2,1)} %param.8) | copy-start | bytes 2064388
  7.2 13.8 %copy-start.2 = (bf16[24,4096]{1,0:T(8,128)(2,1)S(1)}, bf16[24,4096]{1,0:T(8,128)(2,1)}, u32[]{:S(2)}) copy-start(bf16[24,4096]{1,0:T(8,128)(2,1)} %param.7) | copy-start | bytes 589828
  9.6 7.9 %all-to-all-start.2 = ((bf16[2,12,1]{1,2,0:T(2,128)(2,1)}), bf16[2,12,1]{1,2,0:T(2,128)(2,1)S(1)}, u32[]{:S(2)}, u32[]{:S(2)}) async-start(bf16[2,12,1]{1,2,0:T(2,128)(2,1)} %all_to_all.71), calls=%async_computation.3 | async-start | bytes 2048 | tf_op jit(solution)/shard_map/all_to_all | solution.py:66
  17.5 8.6 %all-to-all-start.3 = ((bf16[2,12,4096]{2,1,0:T(8,128)(2,1)}), bf16[2,12,4096]{2,1,0:T(8,128)(2,1)S(1)}, u32[]{:S(2)}, u32[]{:S(2)}) async-start(bf16[2,12,4096]{2,1,0:T(8,128)(2,1)} %all_to_all.62), calls=%async_computation.4 | async-start | bytes 524288 | tf_op jit(solution)/shard_map/all_to_all | solution.py:64
  26.1 8.6 %all-to-all-start = ((bf16[24,4,1024]{2,0,1:T(8,128)(2,1)}), bf16[24,4,1024]{2,0,1:T(8,128)(2,1)S(1)}, u32[]{:S(2)}, u32[]{:S(2)}) async-start(bf16[24,4,1024]{2,0,1:T(8,128)(2,1)} %bitcast.43), calls=%async_computation | async-start | bytes 393216 | tf_op jit(solution)/shard_map/all_to_all | solution.py:29
  30.9 7.6 %copy-start.3 = (bf16[1,16,4096]{2,1,0:T(8,128)(2,1)S(1)}, bf16[1,16,4096]{2,1,0:T(8,128)(2,1)}, u32[]{:S(2)}) copy-start(bf16[1,16,4096]{2,1,0:T(8,128)(2,1)} %param.11) | copy-start | bytes 393220
  34.8 19.7 %all-to-all-start.5 = ((bf16[2,12,14336]{2,1,0:T(8,128)(2,1)}), bf16[2,12,14336]{2,1,0:T(8,128)(2,1)S(1)}, u32[]{:S(2)}, u32[]{:S(2)}) async-start(bf16[2,12,14336]{2,1,0:T(8,128)(2,1)} %all_to_all.68), calls=%async_computation.6 | async-start | bytes 1835008 | tf_op jit(solution)/shard_map/all_to_all | solution.py:65
  38.3 50.9 %all-reduce.4.cloned.1.call-start = ((), (), s32[]{:S(2)}) async-start(), calls=%async_computation.8 | async-start | bytes 917504 | tf_op jit(solution)/shard_map/psum | solution.py:113
  54.5 1.4 copy-start.1
  55.8 125.7 %all-reduce.8.cloned.1.call-start = ((), (), s32[]{:S(2)}) async-start(), calls=%async_computation.10 | async-start | bytes 262144 | tf_op jit(solution)/shard_map/psum | solution.py:116
  57.1 163.9 %reduce-scatter.2.cloned.1.call-start = ((), (), s32[]{:S(2)}) async-start(), calls=%async_computation.7 | async-start | bytes 3440640 | tf_op jit(solution)/shard_map/reduce_scatter | solution.py:37
  70.4 112.7 %all-to-all-start.4 = ((bf16[2,12,14336]{2,1,0:T(8,128)(2,1)}), bf16[2,12,14336]{2,1,0:T(8,128)(2,1)S(1)}, u32[]{:S(2)}, u32[]{:S(2)}) async-start(bf16[2,12,14336]{2,1,0:T(8,128)(2,1)} %all_to_all.65), calls=%async_computation.5 | async-start | bytes 1835008 | tf_op jit(solution)/shard_map/all_to_all | solution.py:106
  74.0 186.8 %all-reduce.6.cloned.1.call-start = ((), (), s32[]{:S(2)}) async-start(), calls=%async_computation.9 | async-start | bytes 917504 | tf_op jit(solution)/shard_map/psum | solution.py:113
  221.0 41.8 %all-to-all-start.1 = ((bf16[2,24,7168]{2,1,0:T(8,128)(2,1)}), bf16[2,24,7168]{2,1,0:T(8,128)(2,1)S(1)}, u32[]{:S(2)}, u32[]{:S(2)}) async-start(bf16[2,24,7168]{2,1,0:T(8,128)(2,1)} %bitcast.48), calls=%async_computation.2 | async-start | bytes 1376256 | tf_op jit(solution)/shard_map/all_to_all | solution.py:45
Sparse Core Ops, SparseCore 0:
  55.9 33.2 all-reduce.3
  93.3 88.1 all-reduce.7
  184.1 36.8 reduce-scatter.1
  223.2 37.5 all-reduce.5
